TPU v7x, 32 devices: a whole 2x2x4 slice. The times are simulated.
32 devices in a mesh: sx: 4 (over x, core), sy: 8 (over z, y).
Axes of the slice: x: 2, y: 2, z: 4, core: 2. Of those that a mesh axis runs over, the one named last changes fastest.
Arguments:
- right_side: float32 [8, 8, 8, 8192], P(None, None, None, ('sx', 'sy')), may hold values from -8 to 8
- stretch: float32 [3, 8192], P(None, ('sx', 'sy')), may hold values from 0.3 to 3
- mass_term: float32 [8192], P(('sx', 'sy')), may hold values from 0.5 to 2
- slot_position: int32 [8192], P(('sx', 'sy')), may hold values from 0 to 255, as said below
- coarse_group: int32 [8192], P(('sx', 'sy')), may hold values from 0 to 511, as said below
Outputs:
- smoothed: float32 [8, 8, 8, 8192], P(None, None, None, ('sx', 'sy'))
- fine_residual: float32 [8, 8, 8, 8192], P(None, None, None, ('sx', 'sy'))
- coarse_rhs: float32 [8, 512], P(None, ('sx', 'sy'))
Inputs may be any that keep to these rules, and one draw needn't show every extreme that they name: `slot_position`: each device's block of 256 entries is a permutation of 0 to 255. `coarse_group`: group k is owned by the device of block index k // 16 (block index i * 8 + j); an element of device (i, j) belongs to a group owned by some device (i, j') of the same first index.
All inputs are finite; a program needn't handle non-finite values.
Results may differ from a plain program's by a relative error of at most 0.00013.
Values sent between devices are 32-bit elements; how exact they have to be, the bound alone decides.
A program may use at most 128 MiB of HBM per device.

v0:
```python
import numpy as np
import jax
import jax.numpy as jnp
from jax import lax
from jax.experimental import pallas as pl
from jax.experimental.pallas import tpu as pltpu
from jax.sharding import PartitionSpec as P

NODES = 8
EY = 2
EZ = 128
GRP_DEV = 16
RELAX = 0.35
ORDER = NODES + 2
F32 = jnp.float32
BF16 = jnp.bfloat16
MESH = pl.DeviceIdType.MESH

WY = EY * NODES + 4
NQ = ORDER * WY
NP = ORDER * ORDER

_m = np.arange(1, ORDER + 1, dtype=np.float64)
_S = np.sqrt(2.0 / (ORDER + 1)) * np.sin(np.pi * np.outer(_m, _m) / (ORDER + 1))
_LAM = 2.0 - 2.0 * np.cos(np.pi * _m / (ORDER + 1))
_C = _S / _S[0:1, :]
_HALF = ORDER // 2

DIRS = [(dx, dy) for dx in (-1, 0, 1) for dy in (-1, 0, 1) if (dx, dy) != (0, 0)]
ND = len(DIRS)


def forward(g):
    a = [g[i] + g[ORDER - 1 - i] for i in range(_HALF)]
    b = [g[i] - g[ORDER - 1 - i] for i in range(_HALF)]
    out = []
    for k in range(ORDER):
        part = a if k % 2 == 0 else b
        total = part[0]
        for i in range(1, _HALF):
            total = total + float(_C[i, k]) * part[i]
        out.append(total)
    return out


def backward(v):
    low, high = [], []
    for i in range(_HALF):
        sums = []
        for parity in (0, 1):
            total = None
            for k in range(parity, ORDER, 2):
                term = v[k] if i == 0 else float(_C[i, k]) * v[k]
                total = term if total is None else total + term
            sums.append(total)
        low.append(sums[0] + sums[1])
        high.append(sums[0] - sums[1])
    return low + high[::-1]


def split3(x):
    hi = x.astype(BF16)
    rest = x - hi.astype(F32)
    mid = rest.astype(BF16)
    low = (rest - mid.astype(F32)).astype(BF16)
    return hi, mid, low


def exact_dot(x, table, contract):
    dims = (((1,), (contract,)), ((), ()))
    parts = [lax.dot_general(s, table, dims, preferred_element_type=F32) for s in split3(x)]
    return parts[0] + (parts[1] + parts[2])


def span_send(d, layers, size, base):
    if d > 0:
        return base + size - (layers - 1), layers
    if d < 0:
        return base - 1, layers
    return base - 1, size + 2


def span_recv(d, layers, size, base):
    if d > 0:
        return base - (layers - 1), layers
    if d < 0:
        return base + size - 1, layers
    return base - 1, size + 2


def slab_shape(d, layers):
    return (
        span_send(d[0], layers, NODES, 1)[1],
        span_send(d[1], layers, EY * NODES, 2)[1],
        NODES,
        EZ,
    )


def make_kernel(n_sx, n_sy):
    def kernel(*refs):
        (rs, stretch, mass, slot, group, tables, sm_out, fr_out, co_out) = refs[:9]
        (perm, cb, cc, cn, cf, rt, F, U, PA, PB, zs, ys, ro, mo, sb, rb) = refs[9:25]
        bufs2 = refs[25 : 25 + ND]
        bufs3 = refs[25 + ND : 25 + 2 * ND]
        (s1, r1, sc, rc, s2, r2, s3, r3, s4, r4) = refs[25 + 2 * ND :]
        i = lax.axis_index("sx")
        j = lax.axis_index("sy")

        def exists(dx, dy):
            ok = None
            for pos, d, size in ((i, dx, n_sx), (j, dy, n_sy)):
                cond = pos < size - 1 if d > 0 else (pos > 0 if d < 0 else None)
                if cond is not None:
                    ok = cond if ok is None else jnp.logical_and(ok, cond)
            return ok

        lane = lax.broadcasted_iota(jnp.int32, (8, EZ), 1)
        sub = lax.broadcasted_iota(jnp.int32, (8, EZ), 0)
        zero_tile = jnp.zeros((8, EZ), F32)

        def from_below(v):
            return jnp.where(lane == 0, 0.0, pltpu.roll(v, 1, 1))

        def from_above(v):
            return jnp.where(lane == EZ - 1, 0.0, pltpu.roll(v, EZ - 1, 1))

        for y in range(WY):
            F[0, y] = zero_tile
            F[ORDER - 1, y] = zero_tile
        for x in range(1, ORDER - 1):
            for y in (0, 1, WY - 2, WY - 1):
                F[x, y] = zero_tile
        for n in range(ND):
            cn[n] = zero_tile

        barrier = pltpu.get_barrier_semaphore()
        count = n_sy - 1
        for d in range(1, n_sy):
            pl.semaphore_signal(
                barrier, inc=1, device_id=(i, lax.rem(j + d, n_sy)), device_id_type=MESH
            )
        for dx, dy in DIRS:
            if dx == 0:
                continue
            ok = exists(dx, dy)
            count = count + ok.astype(jnp.int32)

            @pl.when(ok)
            def _():
                pl.semaphore_signal(
                    barrier, inc=1, device_id=(i + dx, j + dy), device_id_type=MESH
                )

        positions = lax.broadcasted_iota(jnp.int32, (EY * EZ, EY * EZ), 0)
        perm[...] = jnp.where(positions == slot[...], 1.0, 0.0).astype(BF16)
        table = perm[...]
        cb[...] = jnp.zeros_like(cb)
        cb[0:3, :] = stretch[...]
        cb[3:4, :] = mass[...]
        ordered = exact_dot(cb[...], table, 1)
        cc[0:4, :] = ordered[0:4, 0:EZ]
        cc[4:8, :] = ordered[0:4, EZ : 2 * EZ]
        Fr = F.reshape(NQ * 8, EZ)
        Ur = U.reshape((ORDER + 2) * WY * 8, EZ)
        for x in range(NODES):
            got = exact_dot(rs[x * 64 : x * 64 + 64, :], perm[...], 1)
            start = ((x + 1) * WY + 2) * 8
            Fr[start : start + 64, :] = got[:, 0:EZ]
            Fr[start + 64 : start + 128, :] = got[:, EZ : 2 * EZ]

        pl.semaphore_wait(barrier, count)

        def edge(d, size, base, sending):
            if d > 0:
                return pl.ds(base + size - 1 if sending else base - 1, 1)
            if d < 0:
                return pl.ds(base if sending else base + size, 1)
            return pl.ds(base, size)

        def copies1(n):
            dx, dy = DIRS[n]
            target = (i + dx, j + dy)
            field = pltpu.make_async_remote_copy(
                src_ref=F.at[edge(dx, NODES, 1, True), edge(dy, EY * NODES, 2, True)],
                dst_ref=F.at[edge(dx, NODES, 1, False), edge(dy, EY * NODES, 2, False)],
                send_sem=s1.at[n],
                recv_sem=r1.at[n],
                device_id=target,
                device_id_type=MESH,
            )
            coeff = pltpu.make_async_remote_copy(
                src_ref=cc,
                dst_ref=cn.at[n],
                send_sem=sc.at[n],
                recv_sem=rc.at[n],
                device_id=target,
                device_id_type=MESH,
            )
            return field, coeff

        def slab_copy(n, source, bufs, layers, ssem, rsem):
            dx, dy = DIRS[n]
            x0, nx = span_send(dx, layers, NODES, 1)
            y0, ny = span_send(dy, layers, EY * NODES, 2)
            return [
                pltpu.make_async_remote_copy(
                    src_ref=source.at[pl.ds(x0, nx), pl.ds(y0, ny)],
                    dst_ref=bufs[n],
                    send_sem=ssem.at[n],
                    recv_sem=rsem.at[n],
                    device_id=(i + dx, j + dy),
                    device_id_type=MESH,
                )
            ]

        def start_all(make):
            for n, (dx, dy) in enumerate(DIRS):

                @pl.when(exists(dx, dy))
                def _():
                    for copy in make(n):
                        copy.start()

        def wait_sends(make):
            for n, (dx, dy) in enumerate(DIRS):

                @pl.when(exists(dx, dy))
                def _():
                    for copy in make(n):
                        copy.wait_send()

        start_all(copies1)

        @pl.loop(0, 2 * NP // 8)
        def _(t):
            row = pl.multiple_of(t * 8, 8)
            upper = row + sub >= NP
            part = [jnp.where(upper, cc[4 + c : 5 + c, :], cc[c : c + 1, :]) for c in range(4)]
            scale = tables[pl.ds(4 * NP + row, 8), :]
            base = (
                part[1] * tables[pl.ds(row, 8), :]
                + part[2] * tables[pl.ds(2 * NP + row, 8), :]
                + part[3]
            )
            for k in range(ORDER):
                rt[pl.ds(pl.multiple_of(t * (8 * ORDER) + 8 * k, 8), 8), :] = (
                    scale * float(_S[0, k] ** 2)
                ) / (base + part[0] * float(_LAM[k]))

        for n, (dx, dy) in enumerate(DIRS):

            @pl.when(exists(-dx, -dy))
            def _():
                for copy in copies1(n):
                    copy.wait_recv()

        for c in range(4):

            def row_of(dx, dy, e):
                if (dx, dy) == (0, 0):
                    return cc[4 * e + c : 4 * e + c + 1, :]
                return cn[DIRS.index((-dx, -dy)), 4 * e + c : 4 * e + c + 1, :]

            for xs, dx in (((0,), -1), (range(1, ORDER - 1), 0), ((ORDER - 1,), 1)):
                first = row_of(dx, -1, 1)
                last = row_of(dx, 1, 0)
                low = jnp.broadcast_to(row_of(dx, 0, 0), (8, EZ))
                high = jnp.broadcast_to(row_of(dx, 0, 1), (8, EZ))
                for x in xs:
                    at = c * NQ + x * WY
                    cf[at : at + 1, :] = jnp.zeros((1, EZ), F32)
                    cf[at + 1 : at + 2, :] = first
                    cf[at + 2 : at + 10, :] = low
                    cf[at + 10 : at + 18, :] = high
                    cf[at + 18 : at + 19, :] = last
                    cf[at + 19 : at + 20, :] = jnp.zeros((1, EZ), F32)

        def load_z(ref, row):
            return [ref[pl.ds(row * 8 + z, 8, stride=8), :] for z in range(NODES)]

        def residual(f, q, coef):
            u = load_z(Ur, q + WY)
            xa, xb = load_z(Ur, q), load_z(Ur, q + 2 * WY)
            ya, yb = load_z(Ur, q + WY - 1), load_z(Ur, q + WY + 1)
            line = [from_below(u[-1])] + u + [from_above(u[0])]
            cx, cy, cz, m = coef
            diag = 2.0 * (cx + cy + cz) + m
            return [
                f[z]
                - (
                    diag * u[z]
                    - cx * (xa[z] + xb[z])
                    - cy * (ya[z] + yb[z])
                    - cz * (line[z] + line[z + 2])
                )
                for z in range(NODES)
            ]

        def solve(first, out):
            outr = out.reshape(NQ * 8, EZ)

            @pl.loop(0, NQ // 8)
            def _(t):
                q = pl.multiple_of(t * 8, 8)
                g = load_z(Fr, q)
                if not first:
                    g = residual(g, q, [cf[pl.ds(c * NQ + q, 8), :] for c in range(4)])
                v = forward([from_below(g[-1])] + g + [from_above(g[0])])
                for k in range(ORDER):
                    zs[pl.ds(pl.multiple_of(k * NQ + q, 8), 8), :] = v[k]

            @pl.loop(0, 13)
            def _(t):
                p = jnp.minimum(t * 8, NP - 8)
                rows = [zs[pl.ds(p * WY + 1 + y, 8, stride=WY), :] for y in range(WY - 2)]
                for e in range(EY):
                    v = forward(rows[8 * e : 8 * e + ORDER])
                    for k in range(ORDER):
                        ys[pl.ds((e * ORDER + k) * NP + p, 8), :] = v[k]

            @pl.loop(0, 2 * NP // 8)
            def _(t):
                row = t * (8 * ORDER)
                v = forward([ys[pl.ds(row + x, 8, stride=ORDER), :] for x in range(ORDER)])
                v = [
                    v[k] * rt[pl.ds(pl.multiple_of(row + 8 * k, 8), 8), :] for k in range(ORDER)
                ]
                v = backward(v)
                for x in range(ORDER):
                    ys[pl.ds(row + x, 8, stride=ORDER), :] = v[x]

            @pl.loop(0, 13)
            def _(t):
                p = jnp.minimum(t * 8, NP - 8)
                a = backward([ys[pl.ds(k * NP + p, 8), :] for k in range(ORDER)])
                b = backward([ys[pl.ds((ORDER + k) * NP + p, 8), :] for k in range(ORDER)])
                rows = a[:8] + [a[8] + b[0], a[9] + b[1]] + b[2:]
                for y in range(WY - 2):
                    zs[pl.ds(p * WY + 1 + y, 8, stride=WY), :] = rows[y]

            @pl.loop(0, NQ // 8)
            def _(t):
                q = pl.multiple_of(t * 8, 8)
                v = backward([zs[pl.ds(pl.multiple_of(k * NQ + q, 8), 8), :] for k in range(ORDER)])
                body = v[1:-1]
                body[0] = body[0] + from_below(v[-1])
                body[-1] = body[-1] + from_above(v[0])
                for z in range(NODES):
                    outr[pl.ds(q * 8 + z, 8, stride=8), :] = body[z]

            for edge_x, ok in ((0, i > 0), (ORDER - 1, i < n_sx - 1)):

                @pl.when(jnp.logical_not(ok))
                def _():
                    for y in range(WY):
                        out[edge_x, y] = zero_tile

            for edge_y, ok in ((1, j > 0), (WY - 2, j < n_sy - 1)):

                @pl.when(jnp.logical_not(ok))
                def _():
                    for x in range(ORDER):
                        out[x, edge_y] = zero_tile

        def gather(n, make, bufs, layers):
            dx, dy = DIRS[n]

            @pl.when(exists(-dx, -dy))
            def _():
                for copy in make(n):
                    copy.wait_recv()
                x0, nx = span_recv(dx, layers, NODES, 2)
                y0, ny = span_recv(dy, layers, EY * NODES, 2)

                @pl.loop(0, nx)
                def _(x):
                    U[pl.ds(x0 + x, 1), pl.ds(y0, ny)] = (
                        U[pl.ds(x0 + x, 1), pl.ds(y0, ny)] + bufs[n][pl.ds(x, 1)]
                    )

        inner = pl.ds(1, WY - 2)

        @pl.loop(0, ORDER + 2)
        def _(x):
            U[pl.ds(x, 1)] = jnp.zeros((1, WY, 8, EZ), F32)

        solve(True, PA)
        make2 = lambda n: slab_copy(n, PA, bufs2, 3, s2, r2)
        start_all(make2)

        @pl.loop(0, ORDER)
        def _(x):
            U[pl.ds(x + 1, 1), inner] = PA[pl.ds(x, 1), inner]

        for n in range(ND):
            gather(n, make2, bufs2, 3)

        solve(False, PB)
        make3 = lambda n: slab_copy(n, PB, bufs3, 2, s3, r3)
        start_all(make3)

        @pl.loop(0, ORDER)
        def _(x):
            U[pl.ds(x + 1, 1), inner] = U[pl.ds(x + 1, 1), inner] + PB[pl.ds(x, 1), inner]

        for n in range(ND):
            gather(n, make3, bufs3, 2)

        weights = [((NODES - 1 - t) / (NODES - 1), t / (NODES - 1)) for t in range(NODES)]
        coefs = [
            [jnp.broadcast_to(cc[4 * h + c : 4 * h + c + 1, :], (8, EZ)) for c in range(4)]
            for h in range(EY)
        ]

        def last(x, carry):
            wx = x.astype(F32) * (1.0 / (NODES - 1))
            carry = list(carry)
            for h in range(EY):
                q = (x + 1) * WY + 2 + 8 * h
                r = residual(load_z(Fr, q), q, coefs[h])
                for z in range(NODES):
                    ro[pl.ds((x * 16 + 8 * h) * 8 + z, 8, stride=8), :] = r[z]
                for c in range(2):
                    total = None
                    for z in range(NODES):
                        if weights[z][c] == 0.0:
                            continue
                        term = weights[z][c] * r[z]
                        total = term if total is None else total + term
                    carry[4 * h + c] = carry[4 * h + c] + (1.0 - wx) * total
                    carry[4 * h + 2 + c] = carry[4 * h + 2 + c] + wx * total
            return tuple(carry)

        acc = lax.fori_loop(0, NODES, last, tuple([zero_tile] * 8))
        wy1 = sub.astype(F32) * (1.0 / (NODES - 1))
        for h in range(EY):
            for a in range(2):
                for b in range(2):
                    for c in range(2):
                        w = wy1 if b else 1.0 - wy1
                        row = jnp.sum(acc[4 * h + 2 * a + c] * w, axis=0, keepdims=True)
                        v = 4 * a + 2 * b + c
                        mo[v : v + 1, EZ * h : EZ * (h + 1)] = row
        moments = exact_dot(mo[...], perm[...], 0)
        groups = GRP_DEV * n_sy
        column = group[...] - i * groups
        onehot = jnp.where(
            lax.broadcasted_iota(jnp.int32, (groups, EY * EZ), 0) == column, 1.0, 0.0
        ).astype(BF16)
        partial = exact_dot(moments, onehot, 1)
        per = EZ // GRP_DEV
        for d in range(n_sy):
            block = partial[:, (d // per) * EZ : (d // per + 1) * EZ]
            shift = (d % per) * GRP_DEV
            sb[d] = block if shift == 0 else pltpu.roll(block, EZ - shift, 1)

        def copy4(d):
            dest = lax.rem(j + d, n_sy)
            return pltpu.make_async_remote_copy(
                src_ref=sb.at[dest],
                dst_ref=rb.at[d - 1],
                send_sem=s4.at[d - 1],
                recv_sem=r4.at[d - 1],
                device_id=(i, dest),
                device_id_type=MESH,
            )

        for d in range(1, n_sy):
            copy4(d).start()

        @pl.loop(0, NODES)
        def _(x):
            start = pl.multiple_of(((x + 2) * WY + 2) * 8, 8)
            rows = pl.ds(pl.multiple_of(x * 64, 64), 64)
            u = jnp.concatenate([Ur[pl.ds(start, 64), :], Ur[pl.ds(start + 64, 64), :]], axis=1)
            sm_out[rows, :] = exact_dot(u, perm[...], 0)
            at = pl.multiple_of(x * 128, 128)
            r = jnp.concatenate([ro[pl.ds(at, 64), :], ro[pl.ds(at + 64, 64), :]], axis=1)
            fr_out[rows, :] = exact_dot(r, perm[...], 0)

        wait_sends(copies1)
        wait_sends(make2)
        wait_sends(make3)
        total = sb[j]
        for d in range(1, n_sy):
            copy4(d).wait()
            total = total + rb[d - 1]
        co_out[...] = total[:, 0:GRP_DEV]

    return kernel


def solution(mesh):
    n_sx, n_sy = mesh.shape["sx"], mesh.shape["sy"]
    lam_l = np.tile(np.repeat(_LAM, ORDER), 2)
    lam_k = np.tile(_LAM, 2 * ORDER)
    s0 = _S[0] ** 2
    scale = RELAX * np.tile(np.repeat(s0, ORDER), 2) * np.tile(s0, 2 * ORDER)
    column = np.concatenate([lam_l, lam_k, scale]).astype(np.float32)

    def on_device(right_side, stretch, mass_term, slot_position, coarse_group):
        elements = right_side.shape[3]
        tables = jnp.broadcast_to(jnp.asarray(column)[:, None], (column.size, EZ))
        vmem = pl.BlockSpec(memory_space=pltpu.VMEM)
        V = lambda *shape: pltpu.VMEM(shape, F32)
        dma = lambda n: pltpu.SemaphoreType.DMA((n,))
        points = NODES**3
        scratch = [
            pltpu.VMEM((elements, elements), BF16),
            V(8, elements),
            V(8, EZ),
            V(ND, 8, EZ),
            V(4 * NQ, EZ),
            V(2 * NP * ORDER, EZ),
            V(ORDER, WY, 8, EZ),
            V(ORDER + 2, WY, 8, EZ),
            V(ORDER, WY, 8, EZ),
            V(ORDER, WY, 8, EZ),
            V(ORDER * NQ, EZ),
            V(2 * NP * ORDER, EZ),
            V(2 * points, EZ),
            V(8, elements),
            V(n_sy, 8, EZ),
            V(max(n_sy - 1, 1), 8, EZ),
        ]
        scratch += [V(*slab_shape(d, 3)) for d in DIRS]
        scratch += [V(*slab_shape(d, 2)) for d in DIRS]
        scratch += [dma(ND)] * 8 + [dma(max(n_sy - 1, 1))] * 2
        smoothed, fine, coarse = pl.pallas_call(
            make_kernel(n_sx, n_sy),
            out_shape=(
                jax.ShapeDtypeStruct((points, elements), F32),
                jax.ShapeDtypeStruct((points, elements), F32),
                jax.ShapeDtypeStruct((8, GRP_DEV), F32),
            ),
            in_specs=[vmem] * 6,
            out_specs=(vmem, vmem, vmem),
            scratch_shapes=scratch,
            compiler_params=pltpu.CompilerParams(
                collective_id=0, has_side_effects=True, vmem_limit_bytes=48 * 1024 * 1024
            ),
        )(
            right_side.reshape(points, elements),
            stretch,
            mass_term.reshape(1, elements),
            slot_position.reshape(1, elements),
            coarse_group.reshape(1, elements),
            tables,
        )
        shape = right_side.shape
        return smoothed.reshape(shape), fine.reshape(shape), coarse

    split = ("sx", "sy")
    field = P(None, None, None, split)
    return jax.shard_map(
        on_device,
        mesh=mesh,
        in_specs=(field, P(None, split), P(split), P(split), P(split)),
        out_specs=(field, field, P(None, split)),
        check_vma=False,
    )
```

profile of v0, /device:TPU:0, one launch (start us, length us, event | category | flops | bytes accessed | tf_op | source)
XLA Modules:
  0.0 48.9 jit_solution(7534680143655840324)
XLA Ops:
  0.6 0.0 copy-start.5
  0.6 0.7 %copy-done.5 = f32[600]{0:T(1024)S(1)} copy-done((f32[600]{0:T(1024)S(1)}, f32[600]{0:T(1024)}, u32[]{:S(2)}) %copy-start.5) | copy-done | bytes 2424
  1.3 0.0 copy-start.1
  1.3 0.0 copy-start.2
  1.3 0.0 copy-start.3
  1.3 0.0 copy-start.4
  1.3 0.1 broadcast_in_dim.2.refs_5_
  1.5 0.5 %copy-done.1 = f32[3,256]{1,0:T(4,128)S(1)} copy-done((f32[3,256]{1,0:T(4,128)S(1)}, f32[3,256]{1,0:T(4,128)}, u32[]{:S(2)}) %copy-start.1) | copy-done | bytes 3096
  2.0 0.0 copy-done.2
  2.0 0.0 copy-done.3
  2.0 0.0 copy-done.4
  2.0 0.0 copy-start
  2.1 1.0 %copy-done = f32[8,8,8,256]{3,2,1,0:T(8,128)S(1)} copy-done((f32[8,8,8,256]{3,2,1,0:T(8,128)S(1)}, f32[8,8,8,256]{3,2,1,0:T(8,128)}, u32[]{:S(2)}) %copy-start) | copy-done | bytes 524312
  3.1 43.6 %shard_map.85 = (f32[512,256]{1,0:T(8,128)S(1)}, f32[512,256]{1,0:T(8,128)S(1)}, f32[8,16]{1,0:T(8,128)S(1)}) custom-call(f32[512,256]{1,0:T(8,128)S(1)} %bitcast.6, f32[3,256]{1,0:T(4,128)S(1)} %copy-done.1, f32[1,256]{1,0:T(1,128)S(1)} %bitcast.9, s32[1,256]{1,0:T(1,128)S(1)} %bitcast.10, s32[1,256]{1,0:T(1,128)S(1)} %bitcast.11, ...), custom_call_target="tpu_custom_call" | custom-call | tf_op jit(solution)/shard_map/pallas_call | solution.py:530
  46.7 0.8 %copy.12 = f32[8,8,8,256]{3,2,1,0:T(8,128)} copy(f32[8,8,8,256]{3,2,1,0:T(8,128)S(1)} %bitcast.8) | data formatting | bytes 1048576
  47.5 0.8 %copy.13 = f32[8,8,8,256]{3,2,1,0:T(8,128)} copy(f32[8,8,8,256]{3,2,1,0:T(8,128)S(1)} %bitcast.7) | data formatting | bytes 1048576
  48.3 0.6 %copy.14 = f32[8,16]{1,0:T(8,128)} copy(f32[8,16]{1,0:T(8,128)S(1)} %get-tuple-element.14) | data formatting | bytes 1024
Async XLA Ops:
  0.6 0.7 %copy-start.5 = (f32[600]{0:T(1024)S(1)}, f32[600]{0:T(1024)}, u32[]{:S(2)}) copy-start(f32[600]{0:T(1024)} %constant.2.clone) | copy-start | bytes 7204
  1.3 0.7 %copy-start.1 = (f32[3,256]{1,0:T(4,128)S(1)}, f32[3,256]{1,0:T(4,128)}, u32[]{:S(2)}) copy-start(f32[3,256]{1,0:T(4,128)} %refs_1_.1) | copy-start | bytes 9220
  1.3 0.7 %copy-start.2 = (f32[256]{0:T(256)S(1)}, f32[256]{0:T(256)}, u32[]{:S(2)}) copy-start(f32[256]{0:T(256)} %param.8) | copy-start | bytes 3076
  1.3 0.7 %copy-start.3 = (s32[256]{0:T(256)S(1)}, s32[256]{0:T(256)}, u32[]{:S(2)}) copy-start(s32[256]{0:T(256)} %param.9) | copy-start | bytes 3076
  1.3 0.7 %copy-start.4 = (s32[256]{0:T(256)S(1)}, s32[256]{0:T(256)}, u32[]{:S(2)}) copy-start(s32[256]{0:T(256)} %param.10) | copy-start | bytes 3076
  2.0 1.0 %copy-start = (f32[8,8,8,256]{3,2,1,0:T(8,128)S(1)}, f32[8,8,8,256]{3,2,1,0:T(8,128)}, u32[]{:S(2)}) copy-start(f32[8,8,8,256]{3,2,1,0:T(8,128)} %param.6) | copy-start | bytes 1572868
where the time goes:
time: 49.1 us; the launch traced here: 48.9 us
  Pallas kernels  43.6 us (89%)
  local copies, waits for them, and re-layouts  4.62 us (9%)
  between operations  0.66 us (1%)
    pallas_call x1, Pallas kernels, on_device(): pl.pallas_call(make_kernel(n_sx, n_sy), out_shape=(jax.ShapeDtypeStruct((...  43.6 us
    unnamed x15, local copies, waits for them, and re-layouts  4.48 us

commit v1 on v0

v1 whole, which is shorter than its diff:
```python
import numpy as np
import jax
import jax.numpy as jnp
from jax import lax
from jax.experimental import pallas as pl
from jax.experimental.pallas import tpu as pltpu
from jax.sharding import PartitionSpec as P

NODES = 8
EY = 2
EZ = 128
GRP_DEV = 16
RELAX = 0.35
ORDER = NODES + 2
F32 = jnp.float32
BF16 = jnp.bfloat16
MESH = pl.DeviceIdType.MESH

WY = EY * NODES + 4
LX = NODES * WY
NQ = ORDER * WY
NP = ORDER * ORDER
NT = 13
TY = EY * NODES

_m = np.arange(1, ORDER + 1, dtype=np.float64)
_S = np.sqrt(2.0 / (ORDER + 1)) * np.sin(np.pi * np.outer(_m, _m) / (ORDER + 1))
_LAM = 2.0 - 2.0 * np.cos(np.pi * _m / (ORDER + 1))
_C = _S / _S[0:1, :]
_HALF = ORDER // 2

DIRS = [(dx, dy) for dx in (-1, 0, 1) for dy in (-1, 0, 1) if (dx, dy) != (0, 0)]
ND = len(DIRS)


def forward(g):
    a = [g[i] + g[ORDER - 1 - i] for i in range(_HALF)]
    b = [g[i] - g[ORDER - 1 - i] for i in range(_HALF)]
    out = []
    for k in range(ORDER):
        part = a if k % 2 == 0 else b
        total = part[0]
        for i in range(1, _HALF):
            total = total + float(_C[i, k]) * part[i]
        out.append(total)
    return out


def backward(v):
    low, high = [], []
    for i in range(_HALF):
        sums = []
        for parity in (0, 1):
            total = None
            for k in range(parity, ORDER, 2):
                term = v[k] if i == 0 else float(_C[i, k]) * v[k]
                total = term if total is None else total + term
            sums.append(total)
        low.append(sums[0] + sums[1])
        high.append(sums[0] - sums[1])
    return low + high[::-1]


def split3(x):
    hi = x.astype(BF16)
    rest = x - hi.astype(F32)
    mid = rest.astype(BF16)
    low = (rest - mid.astype(F32)).astype(BF16)
    return hi, mid, low


def exact_dot(x, table, contract):
    dims = (((1,), (contract,)), ((), ()))
    parts = [lax.dot_general(s, table, dims, preferred_element_type=F32) for s in split3(x)]
    return parts[0] + (parts[1] + parts[2])


def edge_range(d, size, layers):
    if d > 0:
        return range(size - layers + 1, size + 1)
    return range(-1, layers - 1)


def slab_messages(layers, early):
    out = []
    for group, dy in ((early, 1 if early else -1), (1 - early, -1 if early else 1)):
        for dx in (0, -1, 1):
            xs = range(-1, NODES + 1) if dx == 0 else edge_range(dx, NODES, layers)
            ys = edge_range(dy, TY, layers)
            far_x = None if dx == 0 else (xs[0] if dx > 0 else xs[-1])
            far_y = ys[0] if dy > 0 else ys[-1]
            tiles = [("v", x, y) for y in ys for x in xs if (x, y) != (far_x, far_y)]
            out.append((dx, dy, group, tiles))
        for dx in (-1, 1):
            xs = edge_range(dx, NODES, layers)
            start = 9 if group else -1
            tiles = [("h", x, z, start) for x in xs for z in range(NODES)]
            if group != early:
                tiles += [("v", x, y) for x in xs for y in (7, 8)]
            out.append((dx, 0, group, tiles))
    return out


def field_messages():
    out = []
    for dx, dy in DIRS:
        xs = range(NODES) if dx == 0 else ((NODES - 1,) if dx > 0 else (0,))
        if dy == 0:
            tiles = [("h", x, z, y) for x in xs for z in range(NODES) for y in (0, 8)]
        else:
            tiles = [("v", x, TY - 1 if dy > 0 else 0) for x in xs]
        out.append((dx, dy, 0, tiles))
    return out


ROUNDS = (field_messages(), slab_messages(3, 1), slab_messages(2, 0))


def message_size(message):
    return len(message[3]) + (1 if message in ROUNDS[0] else 0)


def tile_at(tile, shift_x, shift_y):
    if tile[0] == "v":
        return pl.ds((tile[1] + shift_x) * LX + tile[2] + shift_y, 8, stride=WY)
    return pl.ds(((tile[1] + shift_x) * NODES + tile[2]) * WY + tile[3] + shift_y, 8)


def make_kernel(n_sx, n_sy):
    def kernel(*refs):
        (rs, stretch, mass, slot, group, tables, sm_out, fr_out, co_out) = refs[:9]
        (perm, cb, cc, cn, cf, rt, F, U, PA, zs, zi, ys, yt, ov, ro, mo, sb, rb) = refs[9:27]
        at = 27
        rounds = []
        for messages in ROUNDS:
            n = len(messages)
            rounds.append(
                (messages, refs[at : at + n], refs[at + n : at + 2 * n]) + refs[at + 2 * n : at + 2 * n + 2]
            )
            at += 2 * n + 2
        s4, r4 = refs[at : at + 2]
        i = lax.axis_index("sx")
        j = lax.axis_index("sy")

        def exists(dx, dy):
            ok = None
            for pos, d, size in ((i, dx, n_sx), (j, dy, n_sy)):
                cond = pos < size - 1 if d > 0 else (pos > 0 if d < 0 else None)
                if cond is not None:
                    ok = cond if ok is None else jnp.logical_and(ok, cond)
            return ok

        lane = lax.broadcasted_iota(jnp.int32, (8, EZ), 1)
        sub = lax.broadcasted_iota(jnp.int32, (8, EZ), 0)
        zero_tile = jnp.zeros((8, EZ), F32)

        def from_below(v):
            return jnp.where(lane == 0, 0.0, pltpu.roll(v, 1, 1))

        def from_above(v):
            return jnp.where(lane == EZ - 1, 0.0, pltpu.roll(v, EZ - 1, 1))

        barrier = pltpu.get_barrier_semaphore()
        count = n_sy - 1
        for d in range(1, n_sy):
            pl.semaphore_signal(
                barrier, inc=1, device_id=(i, lax.rem(j + d, n_sy)), device_id_type=MESH
            )
        for dx, dy in DIRS:
            if dx == 0:
                continue
            ok = exists(dx, dy)
            count = count + ok.astype(jnp.int32)

            @pl.when(ok)
            def _():
                pl.semaphore_signal(
                    barrier, inc=1, device_id=(i + dx, j + dy), device_id_type=MESH
                )

        for n in range(ND):
            cn[n] = zero_tile

        positions = lax.broadcasted_iota(jnp.int32, (EY * EZ, EY * EZ), 0)
        perm[...] = jnp.where(positions == slot[...], 1.0, 0.0).astype(BF16)
        cb[...] = jnp.zeros_like(cb)
        cb[0:3, :] = stretch[...]
        cb[3:4, :] = mass[...]
        ordered = exact_dot(cb[...], perm[...], 1)
        cc[0:4, :] = ordered[0:4, 0:EZ]
        cc[4:8, :] = ordered[0:4, EZ : 2 * EZ]
        for x in range(NODES):
            got = exact_dot(rs[x * 64 : x * 64 + 64, :], perm[...], 1)
            for y in range(TY):
                part = got[8 * (y % 8) : 8 * (y % 8) + 8, EZ * (y // 8) : EZ * (y // 8 + 1)]
                F[tile_at(("v", x, y), 1, 2), :] = part

        for x in range(ORDER):
            for y in (range(WY) if x in (0, ORDER - 1) else (0, 1, WY - 2, WY - 1)):
                F[pl.ds(x * LX + y, 8, stride=WY), :] = zero_tile
            for y in (0, WY - 1):
                PA[pl.ds(x * LX + y, 8, stride=WY), :] = zero_tile

        pl.semaphore_wait(barrier, count)

        def copy_of(r, n):
            messages, send, recv, ssem, rsem = rounds[r]
            dx, dy = messages[n][:2]
            return pltpu.make_async_remote_copy(
                src_ref=send[n],
                dst_ref=recv[n],
                send_sem=ssem.at[n],
                recv_sem=rsem.at[n],
                device_id=(i + dx, j + dy),
                device_id_type=MESH,
            )

        def post(r, source, wanted):
            messages, send = rounds[r][:2]
            for n, (dx, dy, g, tiles) in enumerate(messages):
                if not wanted(dx, dy, g):
                    continue

                @pl.when(exists(dx, dy))
                def _():
                    for k, tile in enumerate(tiles):
                        send[n][8 * k : 8 * k + 8, :] = source[tile_at(tile, 1, 2), :]
                    if r == 0:
                        send[n][8 * len(tiles) : 8 * len(tiles) + 8, :] = cc[...]
                    copy_of(r, n).start()

        def collect(r, wanted):
            messages, send, recv = rounds[r][:3]
            for n, (dx, dy, g, tiles) in enumerate(messages):
                if not wanted(dx, dy, g):
                    continue

                @pl.when(exists(-dx, -dy))
                def _():
                    copy_of(r, n).wait_recv()
                    for k, tile in enumerate(tiles):
                        got = recv[n][8 * k : 8 * k + 8, :]
                        if r == 0:
                            F[tile_at(tile, 1 - NODES * dx, 2 - TY * dy), :] = got
                        else:
                            here = tile_at(tile, 2 - NODES * dx, 2 - TY * dy)
                            U[here, :] = U[here, :] + got
                    if r == 0:
                        cn[n] = recv[n][8 * len(tiles) : 8 * len(tiles) + 8, :]

        everything = lambda dx, dy, g: True
        post(0, F, everything)

        for e in range(EY):
            part = [jnp.broadcast_to(cc[4 * e + c : 4 * e + c + 1, :], (8, EZ)) for c in range(4)]

            @pl.loop(0, NT)
            def _(t):
                row = jnp.minimum(t * 8, NP - 8)
                scale = tables[pl.ds(2 * NP + row, 8), :]
                base = (
                    part[1] * tables[pl.ds(row, 8), :]
                    + part[2] * tables[pl.ds(NP + row, 8), :]
                    + part[3]
                )
                for k in range(ORDER):
                    put = pl.multiple_of(((e * NT + t) * ORDER + k) * 8, 8)
                    rt[pl.ds(put, 8), :] = (scale * float(_S[0, k] ** 2)) / (
                        base + part[0] * float(_LAM[k])
                    )

        @pl.loop(0, ORDER + 2)
        def _(x):
            for k in range(LX // 8):
                U[pl.ds(pl.multiple_of(x * LX + 8 * k, 8), 8), :] = zero_tile

        collect(0, everything)

        for c in range(4):

            def row_of(dx, dy, e):
                if (dx, dy) == (0, 0):
                    return cc[4 * e + c : 4 * e + c + 1, :]
                return cn[DIRS.index((-dx, -dy)), 4 * e + c : 4 * e + c + 1, :]

            for xs, dx in (((0,), -1), (range(1, ORDER - 1), 0), ((ORDER - 1,), 1)):
                first = row_of(dx, -1, 1)
                last = row_of(dx, 1, 0)
                low = jnp.broadcast_to(row_of(dx, 0, 0), (8, EZ))
                high = jnp.broadcast_to(row_of(dx, 0, 1), (8, EZ))
                for x in xs:
                    put = c * NQ + x * WY
                    cf[put : put + 1, :] = jnp.zeros((1, EZ), F32)
                    cf[put + 1 : put + 2, :] = first
                    cf[put + 2 : put + 10, :] = low
                    cf[put + 10 : put + 18, :] = high
                    cf[put + 18 : put + 19, :] = last
                    cf[put + 19 : put + 20, :] = jnp.zeros((1, EZ), F32)

        def load_z(ref, row):
            return [ref[pl.ds(row + z * WY, 8), :] for z in range(NODES)]

        def residual(x, y, coef):
            f = load_z(F, x * LX + y)
            here = (x + 1) * LX + y
            u = load_z(U, here)
            xa, xb = load_z(U, here - LX), load_z(U, here + LX)
            ya, yb = load_z(U, here - 1), load_z(U, here + 1)
            line = [from_below(u[-1])] + u + [from_above(u[0])]
            cx, cy, cz, m = coef
            diag = 2.0 * (cx + cy + cz) + m
            return [
                f[z]
                - (
                    diag * u[z]
                    - cx * (xa[z] + xb[z])
                    - cy * (ya[z] + yb[z])
                    - cz * (line[z] + line[z + 2])
                )
                for z in range(NODES)
            ]

        ROW_A, ROW_D, ROW_C = 1, 3, 11

        def z_forward(first, x, starts):
            for y in starts:
                if first:
                    g = load_z(F, x * LX + y)
                else:
                    g = residual(x, y, [cf[pl.ds(c * NQ + x * WY + y, 8), :] for c in range(4)])
                v = forward([from_below(g[-1])] + g + [from_above(g[0])])
                for k in range(ORDER):
                    zs[pl.ds(k * NQ + x * WY + y, 8), :] = v[k]

        def z_backward(starts):
            @pl.loop(0, ORDER)
            def _(x):
                for y in starts:
                    v = backward([zi[pl.ds(k * NQ + x * WY + y, 8), :] for k in range(ORDER)])
                    body = v[1:-1]
                    body[0] = body[0] + from_below(v[-1])
                    body[-1] = body[-1] + from_above(v[0])
                    for z in range(NODES):
                        PA[pl.ds(x * LX + z * WY + y, 8), :] = body[z]

            for x, ok in ((0, i > 0), (ORDER - 1, i < n_sx - 1)):

                @pl.when(jnp.logical_not(ok))
                def _():
                    for y in starts:
                        for z in range(NODES):
                            PA[pl.ds(x * LX + z * WY + y, 8), :] = zero_tile

            for y, start, ok in ((1, ROW_A, j > 0), (WY - 2, ROW_C, j < n_sy - 1)):
                if start in starts:

                    @pl.when(jnp.logical_not(ok))
                    def _():
                        for x in range(ORDER):
                            PA[pl.ds(x * LX + y, 8, stride=WY), :] = zero_tile

        def element(e, second):
            @pl.loop(0, NT)
            def _(t):
                p = jnp.minimum(t * 8, NP - 8)
                v = forward(
                    [zs[pl.ds(p * WY + 1 + 8 * e + y, 8, stride=WY), :] for y in range(ORDER)]
                )
                for k in range(ORDER):
                    ys[pl.ds(k * NP + p, 8), :] = v[k]

            @pl.loop(0, NT)
            def _(t):
                row = jnp.minimum(t * 8, NP - 8) * ORDER
                v = forward([ys[pl.ds(row + x, 8, stride=ORDER), :] for x in range(ORDER)])
                table = (e * NT + t) * ORDER * 8
                v = [
                    v[k] * rt[pl.ds(pl.multiple_of(table + 8 * k, 8), 8), :] for k in range(ORDER)
                ]
                v = backward(v)
                for x in range(ORDER):
                    yt[pl.ds(row + x, 8, stride=ORDER), :] = v[x]

            @pl.loop(0, NT)
            def _(t):
                p = jnp.minimum(t * 8, NP - 8)
                v = backward([yt[pl.ds(k * NP + p, 8), :] for k in range(ORDER)])
                shared = (0, 1) if e else (8, 9)
                for y in range(ORDER):
                    if y in shared:
                        spare = pl.ds((y - shared[0]) * NP + p, 8)
                        if not second:
                            ov[spare, :] = v[y]
                            continue
                        v[y] = v[y] + ov[spare, :]
                    zi[pl.ds(p * WY + 1 + 8 * e + y, 8, stride=WY), :] = v[y]

        @pl.loop(0, ORDER)
        def _(x):
            z_forward(True, x, (ROW_A, ROW_D, ROW_C))

        element(1, False)
        z_backward((ROW_C,))
        post(1, PA, lambda dx, dy, g: g == 1)
        element(0, True)
        z_backward((ROW_A, ROW_D))
        post(1, PA, lambda dx, dy, g: g == 0)

        @pl.loop(0, ORDER)
        def _(x):
            for k in range(LX // 8):
                row = pl.multiple_of(x * LX + 8 * k, 8)
                U[pl.ds(row + LX, 8), :] = PA[pl.ds(row, 8), :]

        collect(1, lambda dx, dy, g: g == 1)

        @pl.loop(3, 7)
        def _(x):
            z_forward(False, x, (ROW_A, ROW_D))

        collect(1, lambda dx, dy, g: g == 0 and dy == 0)

        @pl.loop(0, 6)
        def _(t):
            z_forward(False, jnp.where(t < 3, t, t + 4), (ROW_A, ROW_D))

        element(0, False)
        z_backward((ROW_A,))
        post(2, PA, lambda dx, dy, g: g == 0)
        collect(1, lambda dx, dy, g: g == 0 and dy != 0)

        @pl.loop(0, ORDER)
        def _(x):
            z_forward(False, x, (ROW_C,))

        element(1, True)
        z_backward((ROW_D, ROW_C))
        post(2, PA, lambda dx, dy, g: g == 1)

        @pl.loop(0, ORDER)
        def _(x):
            for k in range(LX // 8):
                row = pl.multiple_of(x * LX + 8 * k, 8)
                U[pl.ds(row + LX, 8), :] = U[pl.ds(row + LX, 8), :] + PA[pl.ds(row, 8), :]

        collect(2, lambda dx, dy, g: g == 0)
        collect(2, lambda dx, dy, g: g == 1)

        weights = [((NODES - 1 - t) / (NODES - 1), t / (NODES - 1)) for t in range(NODES)]
        coefs = [
            [jnp.broadcast_to(cc[4 * h + c : 4 * h + c + 1, :], (8, EZ)) for c in range(4)]
            for h in range(EY)
        ]

        def last(x, carry):
            wx = x.astype(F32) * (1.0 / (NODES - 1))
            carry = list(carry)
            for h in range(EY):
                r = residual(x + 1, 2 + 8 * h, coefs[h])
                for z in range(NODES):
                    ro[pl.ds(x * LX + z * WY + 8 * h, 8), :] = r[z]
                for c in range(2):
                    total = None
                    for z in range(NODES):
                        if weights[z][c] == 0.0:
                            continue
                        term = weights[z][c] * r[z]
                        total = term if total is None else total + term
                    carry[4 * h + c] = carry[4 * h + c] + (1.0 - wx) * total
                    carry[4 * h + 2 + c] = carry[4 * h + 2 + c] + wx * total
            return tuple(carry)

        acc = lax.fori_loop(0, NODES, last, tuple([zero_tile] * 8))
        wy1 = sub.astype(F32) * (1.0 / (NODES - 1))
        for h in range(EY):
            for a in range(2):
                for b in range(2):
                    for c in range(2):
                        w = wy1 if b else 1.0 - wy1
                        row = jnp.sum(acc[4 * h + 2 * a + c] * w, axis=0, keepdims=True)
                        v = 4 * a + 2 * b + c
                        mo[v : v + 1, EZ * h : EZ * (h + 1)] = row
        moments = exact_dot(mo[...], perm[...], 0)
        groups = GRP_DEV * n_sy
        column = group[...] - i * groups
        onehot = jnp.where(
            lax.broadcasted_iota(jnp.int32, (groups, EY * EZ), 0) == column, 1.0, 0.0
        ).astype(BF16)
        partial = exact_dot(moments, onehot, 1)
        per = EZ // GRP_DEV
        for d in range(n_sy):
            block = partial[:, (d // per) * EZ : (d // per + 1) * EZ]
            shift = (d % per) * GRP_DEV
            sb[d] = block if shift == 0 else pltpu.roll(block, EZ - shift, 1)

        def copy4(d):
            dest = lax.rem(j + d, n_sy)
            return pltpu.make_async_remote_copy(
                src_ref=sb.at[dest],
                dst_ref=rb.at[d - 1],
                send_sem=s4.at[d - 1],
                recv_sem=r4.at[d - 1],
                device_id=(i, dest),
                device_id_type=MESH,
            )

        for d in range(1, n_sy):
            copy4(d).start()

        def slots(ref, base):
            halves = [
                jnp.concatenate(
                    [ref[pl.ds(base + 8 * h + y, 8, stride=WY), :] for y in range(8)], axis=0
                )
                for h in range(EY)
            ]
            return exact_dot(jnp.concatenate(halves, axis=1), perm[...], 0)

        @pl.loop(0, NODES)
        def _(x):
            rows = pl.ds(pl.multiple_of(x * 64, 64), 64)
            sm_out[rows, :] = slots(U, (x + 2) * LX + 2)
            fr_out[rows, :] = slots(ro, x * LX)

        for r in range(len(ROUNDS)):
            for n, (dx, dy, g, tiles) in enumerate(ROUNDS[r]):

                @pl.when(exists(dx, dy))
                def _():
                    copy_of(r, n).wait_send()

        total = sb[j]
        for d in range(1, n_sy):
            copy4(d).wait()
            total = total + rb[d - 1]
        co_out[...] = total[:, 0:GRP_DEV]

    return kernel


def solution(mesh):
    n_sx, n_sy = mesh.shape["sx"], mesh.shape["sy"]
    s0 = _S[0] ** 2
    column = np.concatenate(
        [np.repeat(_LAM, ORDER), np.tile(_LAM, ORDER), RELAX * np.outer(s0, s0).ravel()]
    ).astype(np.float32)

    def on_device(right_side, stretch, mass_term, slot_position, coarse_group):
        elements = right_side.shape[3]
        tables = jnp.broadcast_to(jnp.asarray(column)[:, None], (column.size, EZ))
        vmem = pl.BlockSpec(memory_space=pltpu.VMEM)
        V = lambda *shape: pltpu.VMEM(shape, F32)
        dma = lambda n: pltpu.SemaphoreType.DMA((n,))
        points = NODES**3
        scratch = [
            pltpu.VMEM((elements, elements), BF16),
            V(8, elements),
            V(8, EZ),
            V(ND, 8, EZ),
            V(4 * NQ, EZ),
            V(EY * NT * ORDER * 8, EZ),
            V(ORDER * LX, EZ),
            V((ORDER + 2) * LX, EZ),
            V(ORDER * LX, EZ),
            V(ORDER * NQ, EZ),
            V(ORDER * NQ, EZ),
            V(ORDER * NP, EZ),
            V(ORDER * NP, EZ),
            V(2 * NP, EZ),
            V(NODES * LX, EZ),
            V(8, elements),
            V(n_sy, 8, EZ),
            V(max(n_sy - 1, 1), 8, EZ),
        ]
        for messages in ROUNDS:
            for side in range(2):
                scratch += [V(8 * message_size(m), EZ) for m in messages]
            scratch += [dma(len(messages))] * 2
        scratch += [dma(max(n_sy - 1, 1))] * 2
        smoothed, fine, coarse = pl.pallas_call(
            make_kernel(n_sx, n_sy),
            out_shape=(
                jax.ShapeDtypeStruct((points, elements), F32),
                jax.ShapeDtypeStruct((points, elements), F32),
                jax.ShapeDtypeStruct((8, GRP_DEV), F32),
            ),
            in_specs=[vmem] * 6,
            out_specs=(vmem, vmem, vmem),
            scratch_shapes=scratch,
            compiler_params=pltpu.CompilerParams(
                collective_id=0, has_side_effects=True, vmem_limit_bytes=48 * 1024 * 1024
            ),
        )(
            right_side.reshape(points, elements),
            stretch,
            mass_term.reshape(1, elements),
            slot_position.reshape(1, elements),
            coarse_group.reshape(1, elements),
            tables,
        )
        shape = right_side.shape
        return smoothed.reshape(shape), fine.reshape(shape), coarse

    split = ("sx", "sy")
    field = P(None, None, None, split)
    return jax.shard_map(
        on_device,
        mesh=mesh,
        in_specs=(field, P(None, split), P(split), P(split), P(split)),
        out_specs=(field, field, P(None, split)),
        check_vma=False,
    )
```

time: 49.1 us -> 43.4 us (0.88)
  Pallas kernels: 43.6 us -> 37.9 us
    pallas_call x1, Pallas kernels: 43.6 us -> 37.9 us  [on_device(): pl.pallas_call(make_kernel(n_sx, n_sy), out_shape=(jax.ShapeDtypeStruct((...]
where the time goes in v1:
time: 43.4 us; the launch traced here: 43.1 us
  Pallas kernels  37.9 us (87%)
  local copies, waits for them, and re-layouts  4.61 us (11%)
  between operations  0.66 us (2%)
    pallas_call x1, Pallas kernels, on_device(): pl.pallas_call(make_kernel(n_sx, n_sy), out_shape=(jax.ShapeDtypeStruct((...  37.9 us
    unnamed x15, local copies, waits for them, and re-layouts  4.52 us

profile of v1, /device:TPU:0, one launch (start us, length us, event | category | flops | bytes accessed | tf_op | source)
XLA Modules:
  0.0 43.1 jit_solution(13336787072497867810)
XLA Ops:
  0.6 0.0 copy-start.5
  0.6 0.7 %copy-done.5 = f32[300]{0:T(512)S(1)} copy-done((f32[300]{0:T(512)S(1)}, f32[300]{0:T(512)}, u32[]{:S(2)}) %copy-start.5) | copy-done | bytes 1224
  1.3 0.0 copy-start.1
  1.3 0.0 copy-start.2
  1.3 0.0 copy-start.3
  1.3 0.0 copy-start.4
  1.3 0.1 broadcast_in_dim.2.refs_5_
  1.4 0.6 %copy-done.1 = f32[3,256]{1,0:T(4,128)S(1)} copy-done((f32[3,256]{1,0:T(4,128)S(1)}, f32[3,256]{1,0:T(4,128)}, u32[]{:S(2)}) %copy-start.1) | copy-done | bytes 3096
  2.0 0.0 copy-done.2
  2.0 0.0 copy-done.3
  2.0 0.0 copy-done.4
  2.0 0.0 copy-start
  2.0 1.0 %copy-done = f32[8,8,8,256]{3,2,1,0:T(8,128)S(1)} copy-done((f32[8,8,8,256]{3,2,1,0:T(8,128)S(1)}, f32[8,8,8,256]{3,2,1,0:T(8,128)}, u32[]{:S(2)}) %copy-start) | copy-done | bytes 524312
  3.1 37.9 %shard_map.85 = (f32[512,256]{1,0:T(8,128)S(1)}, f32[512,256]{1,0:T(8,128)S(1)}, f32[8,16]{1,0:T(8,128)S(1)}) custom-call(f32[512,256]{1,0:T(8,128)S(1)} %bitcast.6, f32[3,256]{1,0:T(4,128)S(1)} %copy-done.1, f32[1,256]{1,0:T(1,128)S(1)} %bitcast.9, s32[1,256]{1,0:T(1,128)S(1)} %bitcast.10, s32[1,256]{1,0:T(1,128)S(1)} %bitcast.11, ...), custom_call_target="tpu_custom_call" | custom-call | tf_op jit(solution)/shard_map/pallas_call | solution.py:580
  40.9 0.8 %copy.12 = f32[8,8,8,256]{3,2,1,0:T(8,128)} copy(f32[8,8,8,256]{3,2,1,0:T(8,128)S(1)} %bitcast.8) | data formatting | bytes 1048576
  41.7 0.8 %copy.13 = f32[8,8,8,256]{3,2,1,0:T(8,128)} copy(f32[8,8,8,256]{3,2,1,0:T(8,128)S(1)} %bitcast.7) | data formatting | bytes 1048576
  42.5 0.6 %copy.14 = f32[8,16]{1,0:T(8,128)} copy(f32[8,16]{1,0:T(8,128)S(1)} %get-tuple-element.14) | data formatting | bytes 1024
Async XLA Ops:
  0.6 0.7 %copy-start.5 = (f32[300]{0:T(512)S(1)}, f32[300]{0:T(512)}, u32[]{:S(2)}) copy-start(f32[300]{0:T(512)} %constant.2.clone) | copy-start | bytes 3604
  1.3 0.7 %copy-start.1 = (f32[3,256]{1,0:T(4,128)S(1)}, f32[3,256]{1,0:T(4,128)}, u32[]{:S(2)}) copy-start(f32[3,256]{1,0:T(4,128)} %refs_1_.1) | copy-start | bytes 9220
  1.3 0.7 %copy-start.2 = (f32[256]{0:T(256)S(1)}, f32[256]{0:T(256)}, u32[]{:S(2)}) copy-start(f32[256]{0:T(256)} %param.8) | copy-start | bytes 3076
  1.3 0.7 %copy-start.3 = (s32[256]{0:T(256)S(1)}, s32[256]{0:T(256)}, u32[]{:S(2)}) copy-start(s32[256]{0:T(256)} %param.9) | copy-start | bytes 3076
  1.3 0.7 %copy-start.4 = (s32[256]{0:T(256)S(1)}, s32[256]{0:T(256)}, u32[]{:S(2)}) copy-start(s32[256]{0:T(256)} %param.10) | copy-start | bytes 3076
  2.0 1.0 %copy-start = (f32[8,8,8,256]{3,2,1,0:T(8,128)S(1)}, f32[8,8,8,256]{3,2,1,0:T(8,128)}, u32[]{:S(2)}) copy-start(f32[8,8,8,256]{3,2,1,0:T(8,128)} %param.6) | copy-start | bytes 1572868

commit v2 on v1

--- a/solution.py
+++ b/solution.py
@@ -128,9 +128,10 @@
 
 def make_kernel(n_sx, n_sy):
     def kernel(*refs):
-        (rs, stretch, mass, slot, group, tables, sm_out, fr_out, co_out) = refs[:9]
-        (perm, cb, cc, cn, cf, rt, F, U, PA, zs, zi, ys, yt, ov, ro, mo, sb, rb) = refs[9:27]
-        at = 27
+        (rs_in, stretch_in, mass_in, slot_in, group_in, sm_out, fr_out, co_out) = refs[:8]
+        (perm, cb, cc, cn, cf, rt, F, U, PA, zs, zi, ys, yt, ov, ro, mo, sb, rb) = refs[8:26]
+        (rs, stretch, mass, slot, group, tables, isem) = refs[26:33]
+        at = 33
         rounds = []
         for messages in ROUNDS:
             n = len(messages)
@@ -139,6 +140,20 @@
             )
             at += 2 * n + 2
         s4, r4 = refs[at : at + 2]
+        loads = [
+            pltpu.make_async_copy(src, dst, isem.at[n])
+            for n, (src, dst) in enumerate(
+                (
+                    (slot_in, slot),
+                    (stretch_in, stretch),
+                    (mass_in, mass),
+                    (rs_in, rs),
+                    (group_in, group),
+                )
+            )
+        ]
+        for load in loads:
+            load.start()
         i = lax.axis_index("sx")
         j = lax.axis_index("sy")
 
@@ -149,16 +164,6 @@
                 if cond is not None:
                     ok = cond if ok is None else jnp.logical_and(ok, cond)
             return ok
-
-        lane = lax.broadcasted_iota(jnp.int32, (8, EZ), 1)
-        sub = lax.broadcasted_iota(jnp.int32, (8, EZ), 0)
-        zero_tile = jnp.zeros((8, EZ), F32)
-
-        def from_below(v):
-            return jnp.where(lane == 0, 0.0, pltpu.roll(v, 1, 1))
-
-        def from_above(v):
-            return jnp.where(lane == EZ - 1, 0.0, pltpu.roll(v, EZ - 1, 1))
 
         barrier = pltpu.get_barrier_semaphore()
         count = n_sy - 1
@@ -178,9 +183,41 @@
                     barrier, inc=1, device_id=(i + dx, j + dy), device_id_type=MESH
                 )
 
+        lane = lax.broadcasted_iota(jnp.int32, (8, EZ), 1)
+        sub = lax.broadcasted_iota(jnp.int32, (8, EZ), 0)
+        zero_tile = jnp.zeros((8, EZ), F32)
+
+        def from_below(v):
+            return jnp.where(lane == 0, 0.0, pltpu.roll(v, 1, 1))
+
+        def from_above(v):
+            return jnp.where(lane == EZ - 1, 0.0, pltpu.roll(v, EZ - 1, 1))
+
         for n in range(ND):
             cn[n] = zero_tile
 
+        for x in range(ORDER):
+            for y in (range(WY) if x in (0, ORDER - 1) else (0, 1, WY - 2, WY - 1)):
+                F[pl.ds(x * LX + y, 8, stride=WY), :] = zero_tile
+            for y in (0, WY - 1):
+                PA[pl.ds(x * LX + y, 8, stride=WY), :] = zero_tile
+
+        @pl.loop(0, ORDER + 2)
+        def _(x):
+            for k in range(LX // 8):
+                U[pl.ds(pl.multiple_of(x * LX + 8 * k, 8), 8), :] = zero_tile
+
+        s0 = _S[0] ** 2
+        for l in range(ORDER):
+            for k in range(ORDER):
+                c = l * ORDER + k
+                values = (_LAM[l], _LAM[k], RELAX * s0[l] * s0[k])
+                for part, value in enumerate(values):
+                    at_row = part * NP + c
+                    tables[at_row : at_row + 1, :] = jnp.full((1, EZ), float(value), F32)
+
+        for load in loads:
+            load.wait()
         positions = lax.broadcasted_iota(jnp.int32, (EY * EZ, EY * EZ), 0)
         perm[...] = jnp.where(positions == slot[...], 1.0, 0.0).astype(BF16)
         cb[...] = jnp.zeros_like(cb)
@@ -195,12 +232,6 @@
                 part = got[8 * (y % 8) : 8 * (y % 8) + 8, EZ * (y // 8) : EZ * (y // 8 + 1)]
                 F[tile_at(("v", x, y), 1, 2), :] = part
 
-        for x in range(ORDER):
-            for y in (range(WY) if x in (0, ORDER - 1) else (0, 1, WY - 2, WY - 1)):
-                F[pl.ds(x * LX + y, 8, stride=WY), :] = zero_tile
-            for y in (0, WY - 1):
-                PA[pl.ds(x * LX + y, 8, stride=WY), :] = zero_tile
-
         pl.semaphore_wait(barrier, count)
 
         def copy_of(r, n):
@@ -247,55 +278,6 @@
                             U[here, :] = U[here, :] + got
                     if r == 0:
                         cn[n] = recv[n][8 * len(tiles) : 8 * len(tiles) + 8, :]
-
-        everything = lambda dx, dy, g: True
-        post(0, F, everything)
-
-        for e in range(EY):
-            part = [jnp.broadcast_to(cc[4 * e + c : 4 * e + c + 1, :], (8, EZ)) for c in range(4)]
-
-            @pl.loop(0, NT)
-            def _(t):
-                row = jnp.minimum(t * 8, NP - 8)
-                scale = tables[pl.ds(2 * NP + row, 8), :]
-                base = (
-                    part[1] * tables[pl.ds(row, 8), :]
-                    + part[2] * tables[pl.ds(NP + row, 8), :]
-                    + part[3]
-                )
-                for k in range(ORDER):
-                    put = pl.multiple_of(((e * NT + t) * ORDER + k) * 8, 8)
-                    rt[pl.ds(put, 8), :] = (scale * float(_S[0, k] ** 2)) / (
-                        base + part[0] * float(_LAM[k])
-                    )
-
-        @pl.loop(0, ORDER + 2)
-        def _(x):
-            for k in range(LX // 8):
-                U[pl.ds(pl.multiple_of(x * LX + 8 * k, 8), 8), :] = zero_tile
-
-        collect(0, everything)
-
-        for c in range(4):
-
-            def row_of(dx, dy, e):
-                if (dx, dy) == (0, 0):
-                    return cc[4 * e + c : 4 * e + c + 1, :]
-                return cn[DIRS.index((-dx, -dy)), 4 * e + c : 4 * e + c + 1, :]
-
-            for xs, dx in (((0,), -1), (range(1, ORDER - 1), 0), ((ORDER - 1,), 1)):
-                first = row_of(dx, -1, 1)
-                last = row_of(dx, 1, 0)
-                low = jnp.broadcast_to(row_of(dx, 0, 0), (8, EZ))
-                high = jnp.broadcast_to(row_of(dx, 0, 1), (8, EZ))
-                for x in xs:
-                    put = c * NQ + x * WY
-                    cf[put : put + 1, :] = jnp.zeros((1, EZ), F32)
-                    cf[put + 1 : put + 2, :] = first
-                    cf[put + 2 : put + 10, :] = low
-                    cf[put + 10 : put + 18, :] = high
-                    cf[put + 18 : put + 19, :] = last
-                    cf[put + 19 : put + 20, :] = jnp.zeros((1, EZ), F32)
 
         def load_z(ref, row):
             return [ref[pl.ds(row + z * WY, 8), :] for z in range(NODES)]
@@ -332,6 +314,54 @@
                 for k in range(ORDER):
                     zs[pl.ds(k * NQ + x * WY + y, 8), :] = v[k]
 
+        everything = lambda dx, dy, g: True
+        post(0, F, everything)
+
+        for e in range(EY):
+            part = [jnp.broadcast_to(cc[4 * e + c : 4 * e + c + 1, :], (8, EZ)) for c in range(4)]
+
+            @pl.loop(0, NT)
+            def _(t):
+                row = jnp.minimum(t * 8, NP - 8)
+                scale = tables[pl.ds(2 * NP + row, 8), :]
+                base = (
+                    part[1] * tables[pl.ds(row, 8), :]
+                    + part[2] * tables[pl.ds(NP + row, 8), :]
+                    + part[3]
+                )
+                for k in range(ORDER):
+                    put = pl.multiple_of(((e * NT + t) * ORDER + k) * 8, 8)
+                    rt[pl.ds(put, 8), :] = (scale * float(_S[0, k] ** 2)) / (
+                        base + part[0] * float(_LAM[k])
+                    )
+
+        @pl.loop(1, ORDER - 1)
+        def _(x):
+            z_forward(True, x, (2, 10))
+
+        collect(0, everything)
+
+        for c in range(4):
+
+            def row_of(dx, dy, e):
+                if (dx, dy) == (0, 0):
+                    return cc[4 * e + c : 4 * e + c + 1, :]
+                return cn[DIRS.index((-dx, -dy)), 4 * e + c : 4 * e + c + 1, :]
+
+            for xs, dx in (((0,), -1), (range(1, ORDER - 1), 0), ((ORDER - 1,), 1)):
+                first = row_of(dx, -1, 1)
+                last = row_of(dx, 1, 0)
+                low = jnp.broadcast_to(row_of(dx, 0, 0), (8, EZ))
+                high = jnp.broadcast_to(row_of(dx, 0, 1), (8, EZ))
+                for x in xs:
+                    put = c * NQ + x * WY
+                    cf[put : put + 1, :] = jnp.zeros((1, EZ), F32)
+                    cf[put + 1 : put + 2, :] = first
+                    cf[put + 2 : put + 10, :] = low
+                    cf[put + 10 : put + 18, :] = high
+                    cf[put + 18 : put + 19, :] = last
+                    cf[put + 19 : put + 20, :] = jnp.zeros((1, EZ), F32)
+
         def z_backward(starts):
             @pl.loop(0, ORDER)
             def _(x):
@@ -395,9 +425,13 @@
                         v[y] = v[y] + ov[spare, :]
                     zi[pl.ds(p * WY + 1 + 8 * e + y, 8, stride=WY), :] = v[y]
 
-        @pl.loop(0, ORDER)
-        def _(x):
+        for x in (0, ORDER - 1):
             z_forward(True, x, (ROW_A, ROW_D, ROW_C))
+        for y in (1, WY - 2):
+            g = [F[pl.ds(LX + z * WY + y, 8, stride=LX), :] for z in range(NODES)]
+            v = forward([from_below(g[-1])] + g + [from_above(g[0])])
+            for k in range(ORDER):
+                zs[pl.ds(k * NQ + WY + y, 8, stride=WY), :] = v[k]
 
         element(1, False)
         z_backward((ROW_C,))
@@ -540,14 +574,8 @@
 
 def solution(mesh):
     n_sx, n_sy = mesh.shape["sx"], mesh.shape["sy"]
-    s0 = _S[0] ** 2
-    column = np.concatenate(
-        [np.repeat(_LAM, ORDER), np.tile(_LAM, ORDER), RELAX * np.outer(s0, s0).ravel()]
-    ).astype(np.float32)
-
     def on_device(right_side, stretch, mass_term, slot_position, coarse_group):
         elements = right_side.shape[3]
-        tables = jnp.broadcast_to(jnp.asarray(column)[:, None], (column.size, EZ))
         vmem = pl.BlockSpec(memory_space=pltpu.VMEM)
         V = lambda *shape: pltpu.VMEM(shape, F32)
         dma = lambda n: pltpu.SemaphoreType.DMA((n,))
@@ -572,6 +600,15 @@
             V(n_sy, 8, EZ),
             V(max(n_sy - 1, 1), 8, EZ),
         ]
+        scratch += [
+            V(points, elements),
+            V(3, elements),
+            V(1, elements),
+            pltpu.VMEM((1, elements), jnp.int32),
+            pltpu.VMEM((1, elements), jnp.int32),
+            V(3 * NP + 4, EZ),
+            dma(5),
+        ]
         for messages in ROUNDS:
             for side in range(2):
                 scratch += [V(8 * message_size(m), EZ) for m in messages]
@@ -584,19 +621,23 @@
                 jax.ShapeDtypeStruct((points, elements), F32),
                 jax.ShapeDtypeStruct((8, GRP_DEV), F32),
             ),
-            in_specs=[vmem] * 6,
+            in_specs=[pl.BlockSpec(memory_space=pltpu.HBM)] * 5,
             out_specs=(vmem, vmem, vmem),
             scratch_shapes=scratch,
             compiler_params=pltpu.CompilerParams(
                 collective_id=0, has_side_effects=True, vmem_limit_bytes=48 * 1024 * 1024
             ),
         )(
-            right_side.reshape(points, elements),
-            stretch,
-            mass_term.reshape(1, elements),
-            slot_position.reshape(1, elements),
-            coarse_group.reshape(1, elements),
-            tables,
+            *(
+                pltpu.with_memory_space_constraint(array, pltpu.HBM)
+                for array in (
+                    right_side.reshape(points, elements),
+                    stretch,
+                    mass_term.reshape(1, elements),
+                    slot_position.reshape(1, elements),
+                    coarse_group.reshape(1, elements),
+                )
+            ),
         )
         shape = right_side.shape
         return smoothed.reshape(shape), fine.reshape(shape), coarse

time: 43.4 us -> 40.5 us (0.933)
  local copies, waits for them, and re-layouts: 4.61 us -> 2.18 us
    unnamed x15 -> x3, local copies, waits for them, and re-layouts: 4.52 us -> 2.18 us
where the time goes in v2:
time: 40.5 us; the launch traced here: 40.3 us
  Pallas kernels  37.5 us (93%)
  local copies, waits for them, and re-layouts  2.18 us (5%)
  between operations  0.64 us (2%)
    pallas_call x1, Pallas kernels, on_device(): pl.pallas_call(make_kernel(n_sx, n_sy), out_shape=(jax.ShapeDtypeStruct((...  37.5 us
    unnamed x3, local copies, waits for them, and re-layouts  2.18 us

profile of v2, /device:TPU:0, one launch (start us, length us, event | category | flops | bytes accessed | tf_op | source)
XLA Modules:
  0.0 40.3 jit_solution(7998080867149328370)
XLA Ops:
  0.6 37.5 %shard_map.76 = (f32[512,256]{1,0:T(8,128)S(1)}, f32[512,256]{1,0:T(8,128)S(1)}, f32[8,16]{1,0:T(8,128)S(1)}) custom-call(f32[512,256]{1,0:T(8,128)} %bitcast.8, f32[3,256]{1,0:T(4,128)} %refs_1_.1, f32[1,256]{1,0:T(1,128)} %bitcast.9, s32[1,256]{1,0:T(1,128)} %bitcast.10, s32[1,256]{1,0:T(1,128)} %bitcast.11), custom_call_target="tpu_custom_call" | custom-call | tf_op jit(solution)/shard_map/pallas_call | solution.py:617
  38.1 0.8 %copy.11 = f32[8,8,8,256]{3,2,1,0:T(8,128)} copy(f32[8,8,8,256]{3,2,1,0:T(8,128)S(1)} %bitcast.7) | data formatting | bytes 1048576
  38.9 0.8 %copy.12 = f32[8,8,8,256]{3,2,1,0:T(8,128)} copy(f32[8,8,8,256]{3,2,1,0:T(8,128)S(1)} %bitcast.6) | data formatting | bytes 1048576
  39.7 0.6 %copy.13 = f32[8,16]{1,0:T(8,128)} copy(f32[8,16]{1,0:T(8,128)S(1)} %get-tuple-element.14) | data formatting | bytes 1024

commit v3 on v2

--- a/solution.py
+++ b/solution.py
@@ -446,17 +446,21 @@
                 row = pl.multiple_of(x * LX + 8 * k, 8)
                 U[pl.ds(row + LX, 8), :] = PA[pl.ds(row, 8), :]
 
+        @pl.loop(3, 7)
+        def _(x):
+            z_forward(False, x, (ROW_D + 1,))
+
         collect(1, lambda dx, dy, g: g == 1)
 
         @pl.loop(3, 7)
         def _(x):
-            z_forward(False, x, (ROW_A, ROW_D))
+            z_forward(False, x, (ROW_A,))
 
         collect(1, lambda dx, dy, g: g == 0 and dy == 0)
 
         @pl.loop(0, 6)
         def _(t):
-            z_forward(False, jnp.where(t < 3, t, t + 4), (ROW_A, ROW_D))
+            z_forward(False, jnp.where(t < 3, t, t + 4), (ROW_A, ROW_D + 1))
 
         element(0, False)
         z_backward((ROW_A,))

time: 40.5 us -> 40.4 us (level)
  no operation moved by 1% of the time
where the time goes in v3:
time: 40.4 us; the launch traced here: 40.2 us
  Pallas kernels  37.4 us (93%)
  local copies, waits for them, and re-layouts  2.18 us (5%)
  between operations  0.64 us (2%)
    pallas_call x1, Pallas kernels, on_device(): pl.pallas_call(make_kernel(n_sx, n_sy), out_shape=(jax.ShapeDtypeStruct((...  37.4 us
    unnamed x3, local copies, waits for them, and re-layouts  2.18 us

profile of v3, /device:TPU:0, one launch (start us, length us, event | category | flops | bytes accessed | tf_op | source)
XLA Modules:
  0.0 40.2 jit_solution(13875445052981450857)
XLA Ops:
  0.6 37.4 %shard_map.76 = (f32[512,256]{1,0:T(8,128)S(1)}, f32[512,256]{1,0:T(8,128)S(1)}, f32[8,16]{1,0:T(8,128)S(1)}) custom-call(f32[512,256]{1,0:T(8,128)} %bitcast.8, f32[3,256]{1,0:T(4,128)} %refs_1_.1, f32[1,256]{1,0:T(1,128)} %bitcast.9, s32[1,256]{1,0:T(1,128)} %bitcast.10, s32[1,256]{1,0:T(1,128)} %bitcast.11), custom_call_target="tpu_custom_call" | custom-call | tf_op jit(solution)/shard_map/pallas_call | solution.py:621
  38.1 0.8 %copy.11 = f32[8,8,8,256]{3,2,1,0:T(8,128)} copy(f32[8,8,8,256]{3,2,1,0:T(8,128)S(1)} %bitcast.7) | data formatting | bytes 1048576
  38.9 0.8 %copy.12 = f32[8,8,8,256]{3,2,1,0:T(8,128)} copy(f32[8,8,8,256]{3,2,1,0:T(8,128)S(1)} %bitcast.6) | data formatting | bytes 1048576
  39.7 0.6 %copy.13 = f32[8,16]{1,0:T(8,128)} copy(f32[8,16]{1,0:T(8,128)S(1)} %get-tuple-element.14) | data formatting | bytes 1024
